TPU v7x, 32 devices: a whole 2x2x4 slice. The times are simulated.
32 devices in a mesh: groups: 2 (over x), pos: 16 (over z, y, core).
Axes of the slice: x: 2, y: 2, z: 4, core: 2. Of those that a mesh axis runs over, the one named last changes fastest.
Arguments:
- activations: bfloat16 [32768, 512], P(('groups', 'pos')), parts along dimension 0, may hold values from -6 to 6
- kernel: bfloat16 [512, 5, 608], P('pos'), may hold values from -0.125 to 0.125
- cotangent: bfloat16 [16384, 608], P(('groups', 'pos')), parts along dimension 0, may hold values from -6 to 6
Outputs:
- pooled: bfloat16 [16384, 608], P(('groups', 'pos')), parts along dimension 0
- input_grad: bfloat16 [32768, 512], P(('groups', 'pos')), parts along dimension 0
- kernel_grad: float32 [1024, 5, 608], P(('groups', 'pos')), parts along dimension 0
There are 2 independent parts, one for each index of `groups`. A program takes and returns all parts, laid end to end along the dimension named above; an argument that names none is the same for every part. Nothing has to cross between parts.
All inputs are finite; a program needn't handle non-finite values.
Results may differ from a plain program's by a relative error of at most 0.0041.
Values may be sent and summed in bfloat16 or wider, within the bound.
A program may use at most 128 MiB of HBM per device.

v0:
```python
import jax
import jax.numpy as jnp
from jax import lax
from jax.sharding import PartitionSpec as P

DILATION_STEP = 4


def extended(cells, sides, width):
    for axis, dim in sides:
        count = lax.axis_size(axis)
        ends = count - 1
        head = lax.slice_in_dim(cells, 0, width, axis=dim)
        tail = lax.slice_in_dim(cells, cells.shape[dim] - width, cells.shape[dim], axis=dim)
        cells = jnp.concatenate(
            [
                lax.ppermute(tail, axis, [(i, (i + 1) % count) for i in range(ends)]),
                cells,
                lax.ppermute(head, axis, [((i + 1) % count, i) for i in range(ends)]),
            ],
            axis=dim,
        )
    return cells


def gelu_value(v):
    return 0.5 * v * (1.0 + jax.scipy.special.erf(v * 0.7071067811865476))


def gelu_slope(v):
    return (
        0.5 * (1.0 + jax.scipy.special.erf(v * 0.7071067811865476))
        + v * jnp.exp(-0.5 * v * v) * 0.3989422804014327
    )


def on_device(activations, kernel, cotangent):
    window_length = activations.shape[0]
    kernel_taps = kernel.shape[1]
    out_width = kernel.shape[2]
    reach_row_count = (kernel_taps - 1) // 2 * DILATION_STEP
    values = activations.astype(jnp.float32)
    gelu = gelu_value(values).astype(jnp.bfloat16)
    padded_activation = extended(gelu, (("pos", 0),), reach_row_count)
    gelu_taps = jnp.stack(
        [
            padded_activation[
                tap_offset * DILATION_STEP : tap_offset * DILATION_STEP + window_length
            ]
            for tap_offset in range(kernel_taps)
        ]
    )
    kernel_full = lax.all_gather(kernel, "pos", axis=0, tiled=True)
    columns = gelu_taps
    dilated_output = jnp.einsum(
        "kpc,cko->po", columns, kernel_full, preferred_element_type=jnp.float32
    )
    pooled = (0.5 * dilated_output.reshape(window_length // 2, 2, out_width).sum(axis=1)).astype(
        jnp.bfloat16
    )
    convolution_gradient = (0.5 * jnp.repeat(cotangent.astype(jnp.float32), 2, axis=0)).astype(
        jnp.bfloat16
    )
    columns = gelu_taps
    kernel_grad = lax.psum_scatter(
        jnp.einsum(
            "kpc,po->cko", columns, convolution_gradient, preferred_element_type=jnp.float32
        ),
        "pos",
        scatter_dimension=0,
        tiled=True,
    )
    padded_gradient = extended(convolution_gradient, (("pos", 0),), reach_row_count)
    grad_taps = jnp.stack(
        [
            padded_gradient[
                (kernel_taps - 1 - tap_offset)
                * DILATION_STEP : (kernel_taps - 1 - tap_offset)
                * DILATION_STEP
                + window_length
            ]
            for tap_offset in range(kernel_taps)
        ]
    )
    block = jnp.einsum("kpo,cko->pc", grad_taps, kernel_full, preferred_element_type=jnp.float32)
    input_grad = (block * gelu_slope(values)).astype(jnp.bfloat16)
    return (pooled, input_grad, kernel_grad)


def solution(mesh):
    placed = (P(("groups", "pos"), None), P("pos", None, None), P(("groups", "pos"), None))
    return jax.shard_map(
        on_device,
        mesh=mesh,
        in_specs=placed,
        out_specs=(
            P(("groups", "pos"), None),
            P(("groups", "pos"), None),
            P(("groups", "pos"), None, None),
        ),
        check_vma=False,
    )
```

profile of v0, /device:TPU:0, one launch (start us, length us, event | category | flops | bytes accessed | tf_op | source)
XLA Modules:
  0.0 191.5 jit_solution(12694590104552449113)
XLA Ops:
  7.2 0.0 copy-start.4
  7.2 0.0 all-gather.2.cloned.1.call-start
  7.2 0.7 all-gather.2.cloned.1.call-update
  7.9 0.0 reduce-scatter.2.cloned.1.call-start
  8.0 1.7 fusion.1
  9.6 1.3 collective-permute-start.1
  10.9 3.0 %collective-permute-start = (bf16[8,512]{1,0:T(8,128)(2,1)S(1)}, bf16[8,512]{1,0:T(8,128)(2,1)S(1)}, u32[]{:S(2)}, u32[]{:S(2)}) collective-permute-start(bf16[8,512]{1,0:T(8,128)(2,1)S(1)} %get-tuple-element.13), channel_id=1, source_target_pairs={{0,1},{1,2},{2,3},{3,4},{4,5},{5,6},{6,7},{7,8},{8,9},{9,10},{10,1... | collective-permute-start | bytes 24584 | tf_op jit(solution)/shard_map/ppermute | solution.py:17
  14.0 0.0 copy-done.4
  14.0 0.3 copy.19
  14.3 0.1 multiply_convert_fusion
  14.4 0.7 broadcast_in_dim.7
  15.1 1.9 convert_element_type.38
  17.0 0.0 collective-permute-done
  17.0 0.1 fusion.25
  17.1 0.2 fusion.29
  17.3 0.9 copy-done.2
  18.2 0.4 bitcast_dynamic-update-slice_fusion
  18.7 0.0 collective-permute-done.1
  18.7 0.2 fusion.22
  18.9 0.1 fusion.27
  19.0 2.3 %copy-done.5 = bf16[5,1024,512]{2,1,0:T(8,128)(2,1)} copy-done((bf16[5,1024,512]{2,1,0:T(8,128)(2,1)}, bf16[5,1024,512]{2,1,0:T(8,128)(2,1)S(1)}, u32[]{:S(2)}) %copy-start.5) | copy-done | bytes 5242904
  21.3 5.4 %convolution_bitcast_fusion = f32[512,5,608]{0,2,1:T(8,128)} fusion(bf16[5,1024,512]{2,1,0:T(8,128)(2,1)S(1)} %fusion.27, bf16[1024,608]{1,0:T(8,128)(2,1)S(1)} %copy-done), kind=kOutput, calls=%fused_computation.5 | convolution fusion | flops 3187671040 | bytes 12713984 | tf_op jit(solution)/shard_map/kpc,po->cko/dot_general | solution.py:66
  26.7 10.9 %copy.26 = f32[512,5,608]{2,1,0:T(8,128)} copy(f32[512,5,608]{0,2,1:T(8,128)} %convolution_bitcast_fusion) | data formatting | bytes 12451840 | tf_op jit(solution)/shard_map/kpc,po->cko/transpose | solution.py:66
  37.6 0.0 reduce-scatter.2.cloned.1.call-update
  37.7 0.8 copy.20
  38.5 1.3 collective-permute-start.2
  39.8 0.8 copy.22
  40.6 5.3 %collective-permute-start.3 = (bf16[8,608]{0,1:T(8,128)(2,1)}, bf16[8,608]{0,1:T(8,128)(2,1)S(1)}, u32[]{:S(2)}, u32[]{:S(2)}) collective-permute-start(bf16[8,608]{0,1:T(8,128)(2,1)} %copy.22), channel_id=1, source_target_pairs={{0,1},{1,2},{2,3},{3,4},{4,5},{5,6},{6,7},{7,8},{8,9},{9,10},{10,1... | collective-permute-start | bytes 29192 | tf_op jit(solution)/shard_map/ppermute | solution.py:17
  45.9 1.9 convert_element_type.39
  47.8 0.6 copy.21
  48.5 1.6 copy.24
  50.1 0.0 collective-permute-done.2
  50.1 2.5 %fusion.15 = bf16[5,1024,608]{1,2,0:T(8,128)(2,1)} fusion(bf16[1024,608]{0,1:T(8,128)(2,1)S(1)} %copy.21, bf16[8,608]{0,1:T(8,128)(2,1)} %collective-permute-done.2), kind=kLoop, calls=%fused_computation.28 | loop fusion | flops 2490367 | bytes 2500096
  52.6 2.7 %fusion.19 = bf16[5,1024,608]{1,2,0:T(8,128)(2,1)} fusion(bf16[5,1024,608]{1,2,0:T(8,128)(2,1)} %fusion.15, bf16[8,608]{0,1:T(8,128)(2,1)} %collective-permute-done.2, bf16[1024,608]{0,1:T(8,128)(2,1)S(1)} %copy.21), kind=kLoop, calls=%fused_computation.34 | loop fusion | flops 2490368 | bytes 2646016
  55.3 1.1 constant_dynamic-update-slice_fusion
  56.4 0.0 collective-permute-done.3
  56.4 1.7 fusion.12
  58.1 1.7 fusion.17
  59.8 0.7 all-gather.2.cloned.1.call-done
  60.5 9.3 %convolution_bitcast_fusion.1 = f32[1024,608]{1,0:T(8,128)} fusion(bf16[5,1024,512]{2,1,0:T(8,128)(2,1)} %copy-done.5, bf16[512,5,608]{2,0,1:T(8,128)(2,1)} %all-gather.2.cloned.1.call-done), kind=kOutput, calls=%fused_computation.15 | convolution fusion | flops 3187671040 | bytes 10846208 | tf_op jit(solution)/shard_map/kpc,cko->po/dot_general | solution.py:55
  69.8 3.5 %reshape.31 = f32[512,2,608]{2,1,0:T(2,128)S(1)} reshape(f32[1024,608]{1,0:T(8,128)} %convolution_bitcast_fusion.1) | data formatting | bytes 4980736 | tf_op jit(solution)/shard_map/reshape | solution.py:58
  73.3 4.6 %reduce_sum.9 = f32[512,608]{1,0:T(8,128)} reduce(f32[512,2,608]{2,1,0:T(2,128)S(1)} %reshape.31, f32[]{:T(128)} %constant.1.clone.1), dimensions={1}, to_apply=%region_0.0 | reduce | flops 311296 | bytes 3735556 | tf_op jit(solution)/shard_map/reduce_sum | solution.py:58
  77.9 1.7 multiply_convert_fusion.1
  79.6 1.1 copy.27
  80.6 0.0 copy-done.3
  80.7 10.2 %fusion.8 = bf16[1024,512]{1,0:T(8,128)(2,1)} fusion(bf16[1024,512]{1,0:T(8,128)(2,1)S(1)} %copy-done.3, bf16[5,1024,608]{1,2,0:T(8,128)(2,1)} %fusion.17, bf16[512,5,608]{2,0,1:T(8,128)(2,1)} %all-gather.2.cloned.1.call-done), kind=kOutput, calls=%fused_computation.14 | convolution fusion | flops 3193438208 | bytes 11436032 | tf_op jit(solution)/shard_map/kpo,cko->pc/dot_general | solution.py:85
  90.8 92.0 %reduce-scatter.2.cloned.1.call-done = f32[32,5,608]{2,1,0:T(8,128)} async-done(((f32[512,5,608]{2,1,0:T(8,128)}), f32[32,5,608]{2,1,0:T(8,128)}) %reduce-scatter.2.cloned.1.call-update) | async-done | bytes 389136 | tf_op jit(solution)/shard_map/reduce_scatter | solution.py:65
  182.8 1.9 %copy.28 = f32[32,5,608]{2,0,1:T(8,128)} copy(f32[32,5,608]{2,1,0:T(8,128)} %reduce-scatter.2.cloned.1.call-done) | data formatting | bytes 778240
  (13 shorter events, 0.1 us)
Async XLA Ops:
  7.2 6.8 %copy-start.4 = (bf16[512,608]{0,1:T(8,128)(2,1)S(1)}, bf16[512,608]{0,1:T(8,128)(2,1)}, u32[]{:S(2)}) copy-start(bf16[512,608]{0,1:T(8,128)(2,1)} %param.5) | copy-start | bytes 1867780
  7.2 53.4 %all-gather.2.cloned.1.call-start = ((), (), s32[]{:S(2)}) async-start(), calls=%async_computation.1 | async-start | bytes 3481600 | tf_op jit(solution)/shard_map/all_gather | solution.py:53
  7.9 174.9 %reduce-scatter.2.cloned.1.call-start = ((), (), s32[]{:S(2)}) async-start(), calls=%async_computation.2 | async-start | bytes 11141120 | tf_op jit(solution)/shard_map/reduce_scatter | solution.py:65
  9.6 9.0 %collective-permute-start.1 = (bf16[8,512]{1,0:T(8,128)(2,1)S(1)}, bf16[8,512]{1,0:T(8,128)(2,1)S(1)}, u32[]{:S(2)}, u32[]{:S(2)}) collective-permute-start(bf16[8,512]{1,0:T(8,128)(2,1)S(1)} %get-tuple-element.12), channel_id=1, source_target_pairs={{1,0},{2,1},{3,2},{4,3},{5,4},{6,5},{7,6},{8,7},{9,8},{10,9},{11,1... | collective-permute-start | bytes 24584 | tf_op jit(solution)/shard_map/ppermute | solution.py:19
  10.9 6.1 %collective-permute-start = (bf16[8,512]{1,0:T(8,128)(2,1)S(1)}, bf16[8,512]{1,0:T(8,128)(2,1)S(1)}, u32[]{:S(2)}, u32[]{:S(2)}) collective-permute-start(bf16[8,512]{1,0:T(8,128)(2,1)S(1)} %get-tuple-element.13), channel_id=1, source_target_pairs={{0,1},{1,2},{2,3},{3,4},{4,5},{5,6},{6,7},{7,8},{8,9},{9,10},{10,1... | collective-permute-start | bytes 24584 | tf_op jit(solution)/shard_map/ppermute | solution.py:17
  17.0 1.2 copy-start.2
  18.7 2.7 %copy-start = (bf16[1024,608]{1,0:T(8,128)(2,1)S(1)}, bf16[1024,608]{1,0:T(8,128)(2,1)}, u32[]{:S(2)}) copy-start(bf16[1024,608]{1,0:T(8,128)(2,1)} %convert_element_type.38) | copy-start | bytes 3735556
  19.0 2.3 %copy-start.5 = (bf16[5,1024,512]{2,1,0:T(8,128)(2,1)}, bf16[5,1024,512]{2,1,0:T(8,128)(2,1)S(1)}, u32[]{:S(2)}) copy-start(bf16[5,1024,512]{2,1,0:T(8,128)(2,1)S(1)} %fusion.27) | copy-start | bytes 15728644
  37.6 10.2 %copy-start.1 = (bf16[1024,608]{1,0:T(8,128)(2,1)S(1)}, bf16[1024,608]{1,0:T(8,128)(2,1)}, u32[]{:S(2)}) copy-start(bf16[1024,608]{1,0:T(8,128)(2,1)} %convert_element_type.38) | copy-start | bytes 3735556
  38.5 11.6 %collective-permute-start.2 = (bf16[8,608]{0,1:T(8,128)(2,1)}, bf16[8,608]{0,1:T(8,128)(2,1)}, u32[]{:S(2)}, u32[]{:S(2)}) collective-permute-start(bf16[8,608]{0,1:T(8,128)(2,1)} %copy.20), channel_id=1, source_target_pairs={{1,0},{2,1},{3,2},{4,3},{5,4},{6,5},{7,6},{8,7},{9,8},{10,9},{11,1... | collective-permute-start | bytes 29192 | tf_op jit(solution)/shard_map/ppermute | solution.py:19
  40.6 15.8 %collective-permute-start.3 = (bf16[8,608]{0,1:T(8,128)(2,1)}, bf16[8,608]{0,1:T(8,128)(2,1)S(1)}, u32[]{:S(2)}, u32[]{:S(2)}) collective-permute-start(bf16[8,608]{0,1:T(8,128)(2,1)} %copy.22), channel_id=1, source_target_pairs={{0,1},{1,2},{2,3},{3,4},{4,5},{5,6},{6,7},{7,8},{8,9},{9,10},{10,1... | collective-permute-start | bytes 29192 | tf_op jit(solution)/shard_map/ppermute | solution.py:17
  77.9 2.7 %copy-start.3 = (bf16[1024,512]{1,0:T(8,128)(2,1)S(1)}, bf16[1024,512]{1,0:T(8,128)(2,1)}, u32[]{:S(2)}) copy-start(bf16[1024,512]{1,0:T(8,128)(2,1)} %param.3) | copy-start | bytes 3145732
Sparse Core Ops, SparseCore 0:
  10.3 50.1 all-gather.1
  64.6 118.1 reduce-scatter.1
where the time goes:
time: 192 us
  waiting for transfers between devices  93.4 us (49%)
  local copies, waits for them, and re-layouts  30.4 us (16%)
  matrix products  24.8 us (13%)
  other arithmetic  17.7 us (9%)
  between operations  14.3 us (7%)
  starting transfers between devices  11 us (6%)
    reduce_scatter x1, waiting for transfers between devices, on_device(): lax.psum_scatter(jnp.einsum('kpc,po->cko', columns, convolution_gradient,...  92 us
    transpose x1, local copies, waits for them, and re-layouts, on_device(): jnp.einsum('kpc,po->cko', columns, convolution_gradient, preferred_elemen...  10.9 us
    dot_general x1, matrix products, on_device(): jnp.einsum('kpo,cko->pc', grad_taps, kernel_full, preferred_element_type=...  10.2 us
    dot_general x1, matrix products, on_device(): jnp.einsum('kpc,cko->po', columns, kernel_full, preferred_element_type=jn...  9.26 us
    ppermute x2, starting transfers between devices, extended(): lax.ppermute(tail, axis, [(i, (i + 1) % count) for i in range(ends)])  8.35 us
    unnamed x7, other arithmetic  7.9 us
    unnamed x16, local copies, waits for them, and re-layouts  7.63 us
    convert_element_type x4, local copies, waits for them, and re-layouts, on_device(): (0.5 * jnp.repeat(cotangent.astype(jnp.float32), 2, axis=0)).astype(jnp.b...  6 us
  transfers between devices with their start and end apart: 6, of which 2 were waited for; matrix products, arithmetic and copies ran while one was open for 35% of the time, Pallas kernels for 0%

commit v1 on v0

--- a/solution.py
+++ b/solution.py
@@ -1,6 +1,10 @@
+import functools
+
 import jax
 import jax.numpy as jnp
 from jax import lax
+from jax.experimental import pallas as pl
+from jax.experimental.pallas import tpu as pltpu
 from jax.sharding import PartitionSpec as P
 
 DILATION_STEP = 4
@@ -87,10 +91,286 @@
     return (pooled, input_grad, kernel_grad)
 
 
+MESH = pl.DeviceIdType.MESH
+F32 = jnp.float32
+BF16 = jnp.bfloat16
+PAD = 8
+
+
+def step_kernel(
+    dims,
+    act, kern, cot,
+    pooled, igrad, kgrad,
+    weights, slope, pairs32, g2x, g2t, dx, ds, part, send1, recv1, part2, send2, recv2, send3, recv3,
+    gedge, ghalo, dhalo, spread,
+    own_sem, dh_s, dh_r, gh_s, gh_r,
+    az_s, az_r, ay_s, ay_r, ax_s, ax_r, ac_s, ac_r,
+    r1_s, r1_r, r2_s, r2_r, r3_s, r3_r,
+):
+    n, A, taps, rows, T2, cin, cout = dims
+    step = DILATION_STEP // 2
+    mid = (taps - 1) // 2
+    g = lax.axis_index("groups")
+    p = lax.axis_index("pos")
+    c = p % 2
+    y = (p // 2) % 2
+    z = p // 4
+
+    def copy(src, dst, ssem, rsem, to):
+        return pltpu.make_async_remote_copy(
+            src_ref=src, dst_ref=dst, send_sem=ssem, recv_sem=rsem, device_id=to, device_id_type=MESH
+        )
+
+    def at(zz, yy, cc):
+        return (g, zz * 4 + yy * 2 + cc)
+
+    core_peer, y_peer, x_peer = at(z, y, 1 - c), at(z, 1 - y, c), (1 - g, p)
+    left, right = (g, (p + n - 1) % n), (g, (p + 1) % n)
+
+    barrier = pltpu.get_barrier_semaphore()
+    for d in range(1, n):
+        pl.semaphore_signal(barrier, inc=1, device_id=(g, (p + d) % n), device_id_type=MESH)
+    pl.semaphore_signal(barrier, inc=1, device_id=x_peer, device_id_type=MESH)
+    pl.semaphore_wait(barrier, n)
+
+    own = pltpu.make_async_copy(kern, weights.at[:, z, y, c], own_sem)
+    own.start()
+
+    dl = copy(cot.at[pl.ds(0, 16)], dhalo.at[1], dh_s.at[0], dh_r.at[1], left)
+    dr = copy(cot.at[pl.ds(T2 - 16, 16)], dhalo.at[0], dh_s.at[1], dh_r.at[0], right)
+    dl.start()
+    dr.start()
+
+    pending = []
+
+    def z_gather(i):
+        zz = (z + i) % A
+        return copy(
+            kern.at[:, g], weights.at[:, z, y, c, g], az_s.at[i], az_r.at[z], at(zz, y, c)
+        )
+
+    def y_gather(zz, src):
+        return copy(src, weights.at[:, zz, y, c, g], ay_s.at[zz], ay_r.at[zz], y_peer)
+
+    def x_gather(zz, yy):
+        block = weights.at[:, zz, yy, c, g]
+        return copy(block, block, ax_s.at[zz, yy], ax_r.at[zz, yy], x_peer)
+
+    def core_gather(zz, yy, src):
+        return copy(src, weights.at[:, zz, yy, c], ac_s.at[zz, yy], ac_r.at[zz, yy], core_peer)
+
+    def go(one):
+        one.start()
+        pending.append(one)
+
+    for i in range(1, A):
+        go(z_gather(i))
+    go(y_gather(z, kern.at[:, g]))
+    go(core_gather(z, y, kern))
+
+    tile = pairs32.shape[1]
+
+    def gelu_tile(i, carry):
+        at_row = pl.multiple_of(i * tile, tile)
+        v = act[pl.ds(at_row, tile), :].astype(F32)
+        e = 0.5 * (1.0 + lax.erf(v * 0.7071067811865476))
+        gelu = (v * e).astype(BF16).astype(F32)
+        slope[pl.ds(at_row, tile), :] = e + v * jnp.exp(-0.5 * v * v) * 0.3989422804014327
+        half = pl.multiple_of(i * (tile // 2), tile // 2)
+        for j in range(cin // 128):
+            lanes = slice(j * 128, j * 128 + 128)
+            pairs32[j] = gelu[:, lanes]
+            g2x[pl.ds(PAD + half, tile // 2), lanes] = (
+                pairs32[j, pl.ds(0, tile // 2, stride=2), :]
+                + pairs32[j, pl.ds(1, tile // 2, stride=2), :]
+            )
+        return carry
+
+    lax.fori_loop(0, 2 * T2 // tile, gelu_tile, 0)
+    gedge[0] = g2x[pl.ds(PAD, 16), :].astype(BF16)
+    gedge[1] = g2x[pl.ds(PAD + T2 - 16, 16), :].astype(BF16)
+    gl = copy(gedge.at[0], ghalo.at[1], gh_s.at[0], gh_r.at[1], left)
+    gr = copy(gedge.at[1], ghalo.at[0], gh_s.at[1], gh_r.at[0], right)
+    gl.start()
+    gr.start()
+
+    cols = 128
+    for i in range(cin // cols):
+        g2t[pl.ds(i * cols, cols), :] = g2x[pl.ds(PAD, T2), pl.ds(i * cols, cols)].T.astype(BF16)
+
+    keep_left = (p > 0).astype(F32)
+    keep_right = (p < n - 1).astype(F32)
+    for i in range(T2 // 128):
+        dx[pl.ds(PAD + i * 128, 128), :] = 0.5 * cot[pl.ds(i * 128, 128), :].astype(F32)
+    dl.wait_recv()
+    dr.wait_recv()
+    dx[pl.ds(0, PAD), :] = dhalo[0].astype(F32)[16 - PAD :] * (0.5 * keep_left)
+    dx[pl.ds(PAD + T2, PAD), :] = dhalo[1].astype(F32)[:PAD] * (0.5 * keep_right)
+
+    half_z = A // 2
+    for k in range(taps):
+        ds[k] = dx[pl.ds(PAD - step * (k - mid), T2), :].astype(BF16)
+        for i in range(2):
+            m = cin // 2
+            term = jnp.dot(g2t[pl.ds(i * m, m), :], ds[k], preferred_element_type=F32)
+            term = term.reshape(half_z, 2, 2, rows, cout)
+            part[k, pl.ds(i * half_z, half_z)] = term
+            send1[k, pl.ds(i * half_z, half_z)] = term.astype(BF16)
+        go(copy(send1.at[k, :, :, 1 - c], recv1.at[k], r1_s.at[k], r1_r.at[k], core_peer))
+
+    for k in range(taps):
+        copy(send1.at[k, :, :, c], recv1.at[k], r1_s.at[k], r1_r.at[k], core_peer).wait_recv()
+        for zz in range(A):
+            send2[k, zz] = (part[k, zz, 1 - y, c] + recv1[k, zz, 1 - y].astype(F32)).astype(BF16)
+        go(copy(send2.at[k], recv2.at[k], r2_s.at[k], r2_r.at[k], y_peer))
+        for zz in range(A):
+            part2[k, zz] = part[k, zz, y, c] + recv1[k, zz, y].astype(F32)
+
+    own.wait()
+    for i in range(1, A):
+        zz = (z + i) % A
+        got = weights.at[:, zz, y, c, g]
+        copy(got, got, az_s.at[i], az_r.at[zz], at(zz, y, c)).wait_recv()
+        go(y_gather(zz, got))
+        go(x_gather(zz, y))
+
+    gl.wait_recv()
+    gr.wait_recv()
+    g2x[pl.ds(0, PAD), :] = ghalo[0].astype(F32)[16 - PAD :] * keep_left
+    g2x[pl.ds(PAD + T2, PAD), :] = ghalo[1].astype(F32)[:PAD] * keep_right
+
+    for k in range(taps):
+        copy(send2.at[k], recv2.at[k], r2_s.at[k], r2_r.at[k], y_peer).wait_recv()
+        for zz in range(A):
+            total = part2[k, zz] + recv2[k, zz].astype(F32)
+            part2[k, zz] = total
+            send3[k, zz] = total.astype(BF16)
+        for i in range(1, A):
+            zz = (z + i) % A
+            go(copy(send3.at[k, zz], recv3.at[k, z], r3_s.at[k, i], r3_r.at[k, z], at(zz, y, c)))
+
+    for i in range(A):
+        zz = (z + i) % A
+        got = weights.at[:, zz, 1 - y, c, g]
+        copy(got, got, ay_s.at[zz], ay_r.at[zz], y_peer).wait_recv()
+        go(x_gather(zz, 1 - y))
+
+    for i in range(A):
+        zz = (z + i) % A
+        for yy in (y, 1 - y) if i else (1 - y,):
+            got = weights.at[:, zz, yy, c, 1 - g]
+            copy(got, got, ax_s.at[zz, yy], ax_r.at[zz, yy], x_peer).wait_recv()
+            go(core_gather(zz, yy, weights.at[:, zz, yy, c]))
+
+    for i in range(A):
+        zz = (z + i) % A
+        for yy in (y, 1 - y):
+            got = weights.at[:, zz, yy, 1 - c]
+            copy(got, got, ac_s.at[zz, yy], ac_r.at[zz, yy], core_peer).wait_recv()
+
+    m = spread.shape[1] // 2
+
+    def conv_tile(i, carry):
+        base = pl.multiple_of(i * m, m)
+        total = jnp.zeros((m, cout), F32)
+        grad = jnp.zeros((m, cin), F32)
+        window = g2x[pl.ds(base, m + 2 * PAD), :]
+        for k in range(taps):
+            off = PAD + step * (k - mid)
+            w = weights[k].reshape(cin, cout)
+            total += jnp.dot(
+                window[off : off + m].astype(BF16), w, preferred_element_type=F32
+            )
+            grad += lax.dot_general(
+                ds[k, pl.ds(base, m), :], w, (((1,), (1,)), ((), ())), preferred_element_type=F32
+            )
+        pooled[pl.ds(base, m), :] = (0.5 * total).astype(BF16)
+        for j in range(cin // 128):
+            lanes = slice(j * 128, j * 128 + 128)
+            spread[j, pl.ds(0, m, stride=2), :] = grad[:, lanes]
+            spread[j, pl.ds(1, m, stride=2), :] = grad[:, lanes]
+            at_row = pl.multiple_of(i * 2 * m, 2 * m)
+            igrad[pl.ds(at_row, 2 * m), lanes] = (
+                spread[j] * slope[pl.ds(at_row, 2 * m), lanes]
+            ).astype(BF16)
+        return carry
+
+    lax.fori_loop(0, T2 // m, conv_tile, 0)
+
+    for k in range(taps):
+        total = part2[k, z]
+        for i in range(1, A):
+            zz = (z + i) % A
+            copy(
+                send3.at[k, zz], recv3.at[k, zz], r3_s.at[k, i], r3_r.at[k, zz], at(zz, y, c)
+            ).wait_recv()
+            total = total + recv3[k, zz].astype(F32)
+        kgrad[k] = total
+
+    for one in (dl, dr, gl, gr):
+        one.wait_send()
+    for one in pending:
+        one.wait_send()
+
+
+def on_device_fused(activations, kernel, cotangent):
+    n = lax.axis_size("pos")
+    A = n // 4
+    rows, taps, cout = kernel.shape
+    T2 = cotangent.shape[0]
+    cin = activations.shape[1]
+    dims = (n, A, taps, rows, T2, cin, cout)
+    kern = jnp.transpose(kernel, (1, 0, 2)).reshape(taps, 2, rows // 2, cout)
+    vmem = pl.BlockSpec(memory_space=pltpu.VMEM)
+    DMA = pltpu.SemaphoreType.DMA
+    pooled, igrad, kgrad = pl.pallas_call(
+        functools.partial(step_kernel, dims),
+        out_shape=(
+            jax.ShapeDtypeStruct((T2, cout), BF16),
+            jax.ShapeDtypeStruct((2 * T2, cin), BF16),
+            jax.ShapeDtypeStruct((taps, rows, cout), F32),
+        ),
+        in_specs=[vmem] * 3,
+        out_specs=(vmem,) * 3,
+        scratch_shapes=[
+            pltpu.VMEM((taps, A, 2, 2, 2, rows // 2, cout), BF16),
+            pltpu.VMEM((2 * T2, cin), F32),
+            pltpu.VMEM((cin // 128, 128, 128), F32),
+            pltpu.VMEM((T2 + 2 * PAD, cin), F32),
+            pltpu.VMEM((cin, T2), BF16),
+            pltpu.VMEM((T2 + 2 * PAD, cout), F32),
+            pltpu.VMEM((taps, T2, cout), BF16),
+            pltpu.VMEM((taps, A, 2, 2, rows, cout), F32),
+            pltpu.VMEM((taps, A, 2, 2, rows, cout), BF16),
+            pltpu.VMEM((taps, A, 2, rows, cout), BF16),
+            pltpu.VMEM((taps, A, rows, cout), F32),
+            pltpu.VMEM((taps, A, rows, cout), BF16),
+            pltpu.VMEM((taps, A, rows, cout), BF16),
+            pltpu.VMEM((taps, A, rows, cout), BF16),
+            pltpu.VMEM((taps, A, rows, cout), BF16),
+            pltpu.VMEM((2, 16, cin), BF16),
+            pltpu.VMEM((2, 16, cin), BF16),
+            pltpu.VMEM((2, 16, cout), BF16),
+            pltpu.VMEM((cin // 128, 512, 128), F32),
+            DMA, DMA((2,)), DMA((2,)), DMA((2,)), DMA((2,)),
+            DMA((A,)), DMA((A,)), DMA((A,)), DMA((A,)),
+            DMA((A, 2)), DMA((A, 2)), DMA((A, 2)), DMA((A, 2)),
+            DMA((taps,)), DMA((taps,)), DMA((taps,)), DMA((taps,)),
+            DMA((taps, A)), DMA((taps, A)),
+        ],
+        compiler_params=pltpu.CompilerParams(
+            collective_id=0, has_side_effects=True, vmem_limit_bytes=50 << 20
+        ),
+    )(activations, kern, cotangent)
+    return pooled, igrad, jnp.transpose(kgrad, (1, 0, 2))
+
+
 def solution(mesh):
     placed = (P(("groups", "pos"), None), P("pos", None, None), P(("groups", "pos"), None))
+    n = mesh.shape["pos"]
+    fused = n == 16 and mesh.shape["groups"] == 2
     return jax.shard_map(
-        on_device,
+        on_device_fused if fused else on_device,
         mesh=mesh,
         in_specs=placed,
         out_specs=(

time: 192 us -> 57.9 us (0.30)
  waiting for transfers between devices: 93.4 us -> 0 us
  Pallas kernels: 0 us -> 50.8 us
  matrix products: 24.8 us -> 0 us
  local copies, waits for them, and re-layouts: 30.4 us -> 6.22 us
  other arithmetic: 17.7 us -> 0 us
  between operations: 14.3 us -> 0.68 us
  starting transfers between devices: 11 us -> 0 us
    reduce_scatter x1 -> x0, waiting for transfers between devices: 92 us -> none  [on_device(): lax.psum_scatter(jnp.einsum('kpc,po->cko', columns, convolution_gradient,...]
    pallas_call x0 -> x1, Pallas kernels: none -> 50.8 us  [on_device_fused(): pl.pallas_call(functools.partial(step_kernel, dims), out_shape=(jax.Shape...]
    dot_general x3 -> x0, matrix products: 24.8 us -> none  [the longest x1 10.2 us: on_device(): jnp.einsum('kpo,cko->pc', grad_taps, kernel_full, preferred_element_type=...]
    ppermute x4 -> x0, starting transfers between devices: 10.9 us -> none  [the longest x2 8.35 us: extended(): lax.ppermute(tail, axis, [(i, (i + 1) % count) for i in range(ends)])]
    transpose x1 -> x0, local copies, waits for them, and re-layouts: 10.9 us -> none  [on_device(): jnp.einsum('kpc,po->cko', columns, convolution_gradient, preferred_elemen...]
    unnamed x7 -> x0, other arithmetic: 7.9 us -> none
    convert_element_type x4 -> x0, local copies, waits for them, and re-layouts: 6 us -> none  [on_device(): (0.5 * jnp.repeat(cotangent.astype(jnp.float32), 2, axis=0)).astype(jnp.b...]
    reduce_sum x1 -> x0, other arithmetic: 4.6 us -> none  [on_device(): dilated_output.reshape(window_length // 2, 2, out_width).sum(axis=1)]
  transfers between devices with their start and end apart: 6 -> 0, of which waited for: 2 -> 0; matrix products, arithmetic and copies ran while one was open for 35% -> 0% of each run, Pallas kernels for 0% -> 0%
where the time goes in v1:
time: 57.9 us; the launch traced here: 57.7 us
  Pallas kernels  50.8 us (88%)
  local copies, waits for them, and re-layouts  6.22 us (11%)
  between operations  0.68 us (1%)
    pallas_call x1, Pallas kernels, on_device_fused(): pl.pallas_call(functools.partial(step_kernel, dims), out_shape=(jax.Shape...  50.8 us
    unnamed x12, local copies, waits for them, and re-layouts  6.22 us

profile of v1, /device:TPU:0, one launch (start us, length us, event | category | flops | bytes accessed | tf_op | source)
XLA Modules:
  0.0 57.7 jit_solution(18048273189853660952)
XLA Ops:
  0.6 0.0 copy-start
  0.6 1.5 %copy.6.cot = bf16[512,608]{1,0:T(8,128)(2,1)S(1)} copy(bf16[512,608]{0,1:T(8,128)(2,1)} %param.5) | data formatting | bytes 1245184 | tf_op args[2]
  2.1 0.0 copy-done
  2.1 0.0 copy-start.3
  2.1 0.9 %copy-done.3 = bf16[32,5,608]{2,0,1:T(8,128)(2,1)S(1)} copy-done((bf16[32,5,608]{2,0,1:T(8,128)(2,1)S(1)}, bf16[32,5,608]{2,0,1:T(8,128)(2,1)}, u32[]{:S(2)}) %copy-start.3) | copy-done | bytes 194584
  3.0 50.8 %shard_map.58 = (bf16[512,608]{1,0:T(8,128)(2,1)S(1)}, bf16[1024,512]{1,0:T(8,128)(2,1)S(1)}, f32[5,32,608]{2,1,0:T(8,128)S(1)}) custom-call(bf16[1024,512]{1,0:T(8,128)(2,1)S(1)} %copy-done, bf16[5,2,16,608]{3,2,1,0:T(8,128)(2,1)S(1)} %bitcast.5, bf16[512,608]{1,0:T(8,128)(2,1)S(1)} %copy.6.cot), custom_call_target="tpu_custom_call" | custom-call | tf_op jit(solution)/shard_map/pallas_call | solution.py:326
  53.8 0.0 copy-start.1
  53.8 0.7 %copy-done.1 = f32[5,32,608]{2,1,0:T(8,128)} copy-done((f32[5,32,608]{2,1,0:T(8,128)}, f32[5,32,608]{2,1,0:T(8,128)S(1)}, u32[]{:S(2)}) %copy-start.1) | copy-done | bytes 389144
  54.6 1.1 %copy.7 = bf16[512,608]{0,1:T(8,128)(2,1)} copy(bf16[512,608]{1,0:T(8,128)(2,1)S(1)} %get-tuple-element.9) | data formatting | bytes 1245184
  55.6 0.0 copy-start.2
  55.6 1.0 %copy.10 = bf16[1024,512]{1,0:T(8,128)(2,1)} copy(bf16[1024,512]{1,0:T(8,128)(2,1)S(1)} %get-tuple-element.16) | data formatting | bytes 2097152
  56.6 0.3 copy-done.2
  56.9 0.8 %copy.11 = f32[32,5,608]{2,0,1:T(8,128)} copy(f32[32,5,608]{2,0,1:T(8,128)S(1)} %bitcast.4) | data formatting | bytes 778240
Async XLA Ops:
  0.6 1.5 %copy-start = (bf16[1024,512]{1,0:T(8,128)(2,1)S(1)}, bf16[1024,512]{1,0:T(8,128)(2,1)}, u32[]{:S(2)}) copy-start(bf16[1024,512]{1,0:T(8,128)(2,1)} %act.1) | copy-start | bytes 3145732
  2.1 0.9 %copy-start.3 = (bf16[32,5,608]{2,0,1:T(8,128)(2,1)S(1)}, bf16[32,5,608]{2,0,1:T(8,128)(2,1)}, u32[]{:S(2)}) copy-start(bf16[32,5,608]{2,0,1:T(8,128)(2,1)} %param.4) | copy-start | bytes 583684
  53.8 0.8 %copy-start.1 = (f32[5,32,608]{2,1,0:T(8,128)}, f32[5,32,608]{2,1,0:T(8,128)S(1)}, u32[]{:S(2)}) copy-start(f32[5,32,608]{2,1,0:T(8,128)S(1)} %get-tuple-element.8) | copy-start | bytes 1167364
  55.6 1.3 %copy-start.2 = (f32[5,32,608]{2,1,0:T(8,128)S(1)}, f32[5,32,608]{2,1,0:T(8,128)}, u32[]{:S(2)}) copy-start(f32[5,32,608]{2,1,0:T(8,128)} %copy-done.1) | copy-start | bytes 1167364

commit v2 on v1

--- a/solution.py
+++ b/solution.py
@@ -102,8 +102,8 @@
     act, kern, cot,
     pooled, igrad, kgrad,
     weights, slope, pairs32, g2x, g2t, dx, ds, part, send1, recv1, part2, send2, recv2, send3, recv3,
-    gedge, ghalo, dhalo, spread,
-    own_sem, dh_s, dh_r, gh_s, gh_r,
+    gedge, ghalo, dhalo, spread, kout,
+    own_sem, out_sem, dh_s, dh_r, gh_s, gh_r,
     az_s, az_r, ay_s, ay_r, ax_s, ax_r, ac_s, ac_r,
     r1_s, r1_r, r2_s, r2_r, r3_s, r3_r,
 ):
@@ -141,16 +141,36 @@
     dl.start()
     dr.start()
 
-    pending = []
-
-    def z_gather(i):
-        zz = (z + i) % A
+    pending, leaving = [], []
+
+    high, low = z // 2, z % 2
+    inner = jnp.logical_and(z > 0, z < A - 1)
+    order = (z, 1 + low * (2 * high - 1), 2 + high * (1 - 2 * low), (A - 1) * (1 - high))
+    onward = (None, z + 1, z - 1, (A - 1) * high)
+
+    def partner(i):
+        return order[i]
+
+    def column(j):
+        return (y, 1 - y)[j]
+
+    def z_gather(src, zz, j, slot, to):
+        yy = column(j)
         return copy(
-            kern.at[:, g], weights.at[:, z, y, c, g], az_s.at[i], az_r.at[z], at(zz, y, c)
+            src, weights.at[:, zz, yy, c, g], az_s.at[slot, j], az_r.at[zz, yy], at(to, y, c)
         )
 
-    def y_gather(zz, src):
-        return copy(src, weights.at[:, zz, y, c, g], ay_s.at[zz], ay_r.at[zz], y_peer)
+    def z_own(src, j, act_on):
+        pl.when(z < A - 1)(lambda: act_on(z_gather(src, z, j, 0, z + 1)))
+        pl.when(z > 0)(lambda: act_on(z_gather(src, z, j, 1, z - 1)))
+
+    def z_onward(i, j, act_on):
+        zz = partner(i)
+        got = weights.at[:, zz, column(j), c, g]
+        pl.when(inner)(lambda: act_on(z_gather(got, zz, j, 1 + i, onward[i])))
+
+    def start(one):
+        one.start()
 
     def x_gather(zz, yy):
         block = weights.at[:, zz, yy, c, g]
@@ -163,9 +183,9 @@
         one.start()
         pending.append(one)
 
-    for i in range(1, A):
-        go(z_gather(i))
-    go(y_gather(z, kern.at[:, g]))
+    y_gather = copy(kern.at[:, g], weights.at[:, z, y, c, g], ay_s, ay_r, y_peer)
+    go(y_gather)
+    z_own(kern.at[:, g], 0, start)
     go(core_gather(z, y, kern))
 
     tile = pairs32.shape[1]
@@ -194,6 +214,73 @@
     gl.start()
     gr.start()
 
+
+    def take_z(i, j):
+        zz, yy = partner(i), column(j)
+        got = weights.at[:, zz, yy, c, g]
+        copy(got, got, az_s.at[1 + i, j], az_r.at[zz, yy], y_peer).wait_recv()
+        z_onward(i, j, start)
+        go(x_gather(zz, yy))
+
+    def take_x(i, yy):
+        zz = partner(i)
+        got = weights.at[:, zz, yy, c, 1 - g]
+        copy(got, got, ax_s.at[zz, yy], ax_r.at[zz, yy], x_peer).wait_recv()
+        go(core_gather(zz, yy, weights.at[:, zz, yy, c]))
+
+    def take_core(i, yy):
+        zz = partner(i)
+        got = weights.at[:, zz, yy, 1 - c]
+        copy(got, got, ac_s.at[zz, yy], ac_r.at[zz, yy], core_peer).wait_recv()
+
+    def tap_dot(k):
+        ds[k] = dx[pl.ds(PAD - step * (k - mid), T2), :].astype(BF16)
+        half_z = A // 2
+        for i in range(2):
+            m = cin // 2
+            term = jnp.dot(g2t[pl.ds(i * m, m), :], ds[k], preferred_element_type=F32)
+            term = term.reshape(half_z, 2, 2, rows, cout)
+            part[k, pl.ds(i * half_z, half_z)] = term
+            send1[k, pl.ds(i * half_z, half_z)] = term.astype(BF16)
+        go(copy(send1.at[k, :, :, 1 - c], recv1.at[k], r1_s.at[k], r1_r.at[k], core_peer))
+
+    def tap_core(k):
+        copy(send1.at[k, :, :, c], recv1.at[k], r1_s.at[k], r1_r.at[k], core_peer).wait_recv()
+        for zz in range(A):
+            send2[k, zz] = (part[k, zz, 1 - y, c] + recv1[k, zz, 1 - y].astype(F32)).astype(BF16)
+        go(copy(send2.at[k], recv2.at[k], r2_s.at[k], r2_r.at[k], y_peer))
+        for zz in range(A):
+            part2[k, zz] = part[k, zz, y, c] + recv1[k, zz, y].astype(F32)
+
+    def tap_y(k):
+        copy(send2.at[k], recv2.at[k], r2_s.at[k], r2_r.at[k], y_peer).wait_recv()
+        for zz in range(A):
+            total = part2[k, zz] + recv2[k, zz].astype(F32)
+            part2[k, zz] = total
+            send3[k, zz] = total.astype(BF16)
+        for i in range(1, A):
+            zz = partner(i)
+            go(copy(send3.at[k, zz], recv3.at[k, z], r3_s.at[k, i], r3_r.at[k, z], at(zz, y, c)))
+
+    def tap_z(k):
+        total = part2[k, z]
+        for i in range(1, A):
+            zz = partner(i)
+            copy(
+                send3.at[k, zz], recv3.at[k, zz], r3_s.at[k, i], r3_r.at[k, zz], at(zz, y, c)
+            ).wait_recv()
+            total = total + recv3[k, zz].astype(F32)
+        kout[k] = total
+        done = pltpu.make_async_copy(kout.at[k], kgrad.at[k], out_sem.at[k])
+        done.start()
+        leaving.append(done)
+
+    own.wait()
+    y_gather.wait_recv()
+    across = weights.at[:, z, 1 - y, c, g]
+    z_own(across, 1, start)
+    go(x_gather(z, 1 - y))
+    take_z(1, 0)
     cols = 128
     for i in range(cin // cols):
         g2t[pl.ds(i * cols, cols), :] = g2x[pl.ds(PAD, T2), pl.ds(i * cols, cols)].T.astype(BF16)
@@ -207,66 +294,33 @@
     dx[pl.ds(0, PAD), :] = dhalo[0].astype(F32)[16 - PAD :] * (0.5 * keep_left)
     dx[pl.ds(PAD + T2, PAD), :] = dhalo[1].astype(F32)[:PAD] * (0.5 * keep_right)
 
-    half_z = A // 2
+
+    arrivals = ((1, 1), (2, 0), (2, 1), (3, 0))
     for k in range(taps):
-        ds[k] = dx[pl.ds(PAD - step * (k - mid), T2), :].astype(BF16)
-        for i in range(2):
-            m = cin // 2
-            term = jnp.dot(g2t[pl.ds(i * m, m), :], ds[k], preferred_element_type=F32)
-            term = term.reshape(half_z, 2, 2, rows, cout)
-            part[k, pl.ds(i * half_z, half_z)] = term
-            send1[k, pl.ds(i * half_z, half_z)] = term.astype(BF16)
-        go(copy(send1.at[k, :, :, 1 - c], recv1.at[k], r1_s.at[k], r1_r.at[k], core_peer))
-
-    for k in range(taps):
-        copy(send1.at[k, :, :, c], recv1.at[k], r1_s.at[k], r1_r.at[k], core_peer).wait_recv()
-        for zz in range(A):
-            send2[k, zz] = (part[k, zz, 1 - y, c] + recv1[k, zz, 1 - y].astype(F32)).astype(BF16)
-        go(copy(send2.at[k], recv2.at[k], r2_s.at[k], r2_r.at[k], y_peer))
-        for zz in range(A):
-            part2[k, zz] = part[k, zz, y, c] + recv1[k, zz, y].astype(F32)
-
-    own.wait()
-    for i in range(1, A):
-        zz = (z + i) % A
-        got = weights.at[:, zz, y, c, g]
-        copy(got, got, az_s.at[i], az_r.at[zz], at(zz, y, c)).wait_recv()
-        go(y_gather(zz, got))
-        go(x_gather(zz, y))
-
+        tap_dot(k)
+        if k:
+            tap_core(k - 1)
+        if k < len(arrivals):
+            take_z(*arrivals[k])
+    tap_core(taps - 1)
+    take_z(3, 1)
     gl.wait_recv()
     gr.wait_recv()
     g2x[pl.ds(0, PAD), :] = ghalo[0].astype(F32)[16 - PAD :] * keep_left
     g2x[pl.ds(PAD + T2, PAD), :] = ghalo[1].astype(F32)[:PAD] * keep_right
-
-    for k in range(taps):
-        copy(send2.at[k], recv2.at[k], r2_s.at[k], r2_r.at[k], y_peer).wait_recv()
-        for zz in range(A):
-            total = part2[k, zz] + recv2[k, zz].astype(F32)
-            part2[k, zz] = total
-            send3[k, zz] = total.astype(BF16)
-        for i in range(1, A):
-            zz = (z + i) % A
-            go(copy(send3.at[k, zz], recv3.at[k, z], r3_s.at[k, i], r3_r.at[k, z], at(zz, y, c)))
-
+    take_x(0, 1 - y)
+    take_x(1, y)
+    take_x(1, 1 - y)
+    tap_y(0)
+    take_x(2, y)
+    take_x(2, 1 - y)
+    tap_y(1)
+    take_x(3, y)
+    take_x(3, 1 - y)
+    tap_y(2)
     for i in range(A):
-        zz = (z + i) % A
-        got = weights.at[:, zz, 1 - y, c, g]
-        copy(got, got, ay_s.at[zz], ay_r.at[zz], y_peer).wait_recv()
-        go(x_gather(zz, 1 - y))
-
-    for i in range(A):
-        zz = (z + i) % A
-        for yy in (y, 1 - y) if i else (1 - y,):
-            got = weights.at[:, zz, yy, c, 1 - g]
-            copy(got, got, ax_s.at[zz, yy], ax_r.at[zz, yy], x_peer).wait_recv()
-            go(core_gather(zz, yy, weights.at[:, zz, yy, c]))
-
-    for i in range(A):
-        zz = (z + i) % A
-        for yy in (y, 1 - y):
-            got = weights.at[:, zz, yy, 1 - c]
-            copy(got, got, ac_s.at[zz, yy], ac_r.at[zz, yy], core_peer).wait_recv()
+        take_core(i, y)
+        take_core(i, 1 - y)
 
     m = spread.shape[1] // 2
 
@@ -297,20 +351,22 @@
 
     lax.fori_loop(0, T2 // m, conv_tile, 0)
 
+    for k in range(3, taps):
+        tap_y(k)
     for k in range(taps):
-        total = part2[k, z]
-        for i in range(1, A):
-            zz = (z + i) % A
-            copy(
-                send3.at[k, zz], recv3.at[k, zz], r3_s.at[k, i], r3_r.at[k, zz], at(zz, y, c)
-            ).wait_recv()
-            total = total + recv3[k, zz].astype(F32)
-        kgrad[k] = total
-
+        tap_z(k)
+
+    for one in leaving:
+        one.wait()
     for one in (dl, dr, gl, gr):
         one.wait_send()
     for one in pending:
         one.wait_send()
+    z_own(kern.at[:, g], 0, lambda one: one.wait_send())
+    z_own(across, 1, lambda one: one.wait_send())
+    for i in range(1, A):
+        for j in range(2):
+            z_onward(i, j, lambda one: one.wait_send())
 
 
 def on_device_fused(activations, kernel, cotangent):
@@ -330,8 +386,8 @@
             jax.ShapeDtypeStruct((2 * T2, cin), BF16),
             jax.ShapeDtypeStruct((taps, rows, cout), F32),
         ),
-        in_specs=[vmem] * 3,
-        out_specs=(vmem,) * 3,
+        in_specs=[vmem, pl.BlockSpec(memory_space=pltpu.HBM), vmem],
+        out_specs=(vmem, vmem, pl.BlockSpec(memory_space=pltpu.HBM)),
         scratch_shapes=[
             pltpu.VMEM((taps, A, 2, 2, 2, rows // 2, cout), BF16),
             pltpu.VMEM((2 * T2, cin), F32),
@@ -352,8 +408,9 @@
             pltpu.VMEM((2, 16, cin), BF16),
             pltpu.VMEM((2, 16, cout), BF16),
             pltpu.VMEM((cin // 128, 512, 128), F32),
-            DMA, DMA((2,)), DMA((2,)), DMA((2,)), DMA((2,)),
-            DMA((A,)), DMA((A,)), DMA((A,)), DMA((A,)),
+            pltpu.VMEM((taps, rows, cout), F32),
+            DMA, DMA((taps,)), DMA((2,)), DMA((2,)), DMA((2,)), DMA((2,)),
+            DMA((A + 1, 2)), DMA((A, 2)), DMA, DMA,
             DMA((A, 2)), DMA((A, 2)), DMA((A, 2)), DMA((A, 2)),
             DMA((taps,)), DMA((taps,)), DMA((taps,)), DMA((taps,)),
             DMA((taps, A)), DMA((taps, A)),

time: 57.9 us -> 50.4 us (0.87)
  Pallas kernels: 50.8 us -> 43.3 us
    pallas_call x1, Pallas kernels: 50.8 us -> 43.3 us  [on_device_fused(): pl.pallas_call(functools.partial(step_kernel, dims), out_shape=(jax.Shape...]
where the time goes in v2:
time: 50.4 us; the launch traced here: 50.2 us
  Pallas kernels  43.3 us (86%)
  local copies, waits for them, and re-layouts  6.22 us (12%)
  between operations  0.68 us (1%)
    pallas_call x1, Pallas kernels, on_device_fused(): pl.pallas_call(functools.partial(step_kernel, dims), out_shape=(jax.Shape...  43.3 us
    unnamed x12, local copies, waits for them, and re-layouts  6.22 us

profile of v2, /device:TPU:0, one launch (start us, length us, event | category | flops | bytes accessed | tf_op | source)
XLA Modules:
  0.0 50.2 jit_solution(3559040057301633970)
XLA Ops:
  0.6 0.0 copy-start
  0.6 1.5 %copy.6.cot = bf16[512,608]{1,0:T(8,128)(2,1)S(1)} copy(bf16[512,608]{0,1:T(8,128)(2,1)} %param.5) | data formatting | bytes 1245184 | tf_op args[2]
  2.1 0.0 copy-done
  2.1 0.0 copy-start.3
  2.1 0.9 %copy-done.3 = bf16[32,5,608]{2,0,1:T(8,128)(2,1)S(1)} copy-done((bf16[32,5,608]{2,0,1:T(8,128)(2,1)S(1)}, bf16[32,5,608]{2,0,1:T(8,128)(2,1)}, u32[]{:S(2)}) %copy-start.3) | copy-done | bytes 194584
  3.0 43.3 %shard_map.58 = (bf16[512,608]{1,0:T(8,128)(2,1)S(1)}, bf16[1024,512]{1,0:T(8,128)(2,1)S(1)}, f32[5,32,608]{2,1,0:T(8,128)S(1)}) custom-call(bf16[1024,512]{1,0:T(8,128)(2,1)S(1)} %copy-done, bf16[5,2,16,608]{3,2,1,0:T(8,128)(2,1)S(1)} %bitcast.5, bf16[512,608]{1,0:T(8,128)(2,1)S(1)} %copy.6.cot), custom_call_target="tpu_custom_call" | custom-call | tf_op jit(solution)/shard_map/pallas_call | solution.py:382
  46.3 0.0 copy-start.1
  46.3 0.7 %copy-done.1 = f32[5,32,608]{2,1,0:T(8,128)} copy-done((f32[5,32,608]{2,1,0:T(8,128)}, f32[5,32,608]{2,1,0:T(8,128)S(1)}, u32[]{:S(2)}) %copy-start.1) | copy-done | bytes 389144
  47.1 1.1 %copy.7 = bf16[512,608]{0,1:T(8,128)(2,1)} copy(bf16[512,608]{1,0:T(8,128)(2,1)S(1)} %get-tuple-element.9) | data formatting | bytes 1245184
  48.2 0.0 copy-start.2
  48.2 1.0 %copy.10 = bf16[1024,512]{1,0:T(8,128)(2,1)} copy(bf16[1024,512]{1,0:T(8,128)(2,1)S(1)} %get-tuple-element.16) | data formatting | bytes 2097152
  49.1 0.3 copy-done.2
  49.4 0.8 %copy.11 = f32[32,5,608]{2,0,1:T(8,128)} copy(f32[32,5,608]{2,0,1:T(8,128)S(1)} %bitcast.4) | data formatting | bytes 778240
Async XLA Ops:
  0.6 1.5 %copy-start = (bf16[1024,512]{1,0:T(8,128)(2,1)S(1)}, bf16[1024,512]{1,0:T(8,128)(2,1)}, u32[]{:S(2)}) copy-start(bf16[1024,512]{1,0:T(8,128)(2,1)} %act.1) | copy-start | bytes 3145732
  2.1 0.9 %copy-start.3 = (bf16[32,5,608]{2,0,1:T(8,128)(2,1)S(1)}, bf16[32,5,608]{2,0,1:T(8,128)(2,1)}, u32[]{:S(2)}) copy-start(bf16[32,5,608]{2,0,1:T(8,128)(2,1)} %param.4) | copy-start | bytes 583684
  46.3 0.8 %copy-start.1 = (f32[5,32,608]{2,1,0:T(8,128)}, f32[5,32,608]{2,1,0:T(8,128)S(1)}, u32[]{:S(2)}) copy-start(f32[5,32,608]{2,1,0:T(8,128)S(1)} %get-tuple-element.8) | copy-start | bytes 1167364
  48.2 1.3 %copy-start.2 = (f32[5,32,608]{2,1,0:T(8,128)S(1)}, f32[5,32,608]{2,1,0:T(8,128)}, u32[]{:S(2)}) copy-start(f32[5,32,608]{2,1,0:T(8,128)} %copy-done.1) | copy-start | bytes 1167364

commit v3 on v2

--- a/solution.py
+++ b/solution.py
@@ -317,7 +317,8 @@
     tap_y(1)
     take_x(3, y)
     take_x(3, 1 - y)
-    tap_y(2)
+    for k in range(2, taps - 1):
+        tap_y(k)
     for i in range(A):
         take_core(i, y)
         take_core(i, 1 - y)
@@ -349,10 +350,10 @@
             ).astype(BF16)
         return carry
 
-    lax.fori_loop(0, T2 // m, conv_tile, 0)
-
-    for k in range(3, taps):
-        tap_y(k)
+    lax.fori_loop(0, 1, conv_tile, 0)
+    tap_y(taps - 1)
+    lax.fori_loop(1, T2 // m, conv_tile, 0)
+
     for k in range(taps):
         tap_z(k)
 

time: 50.4 us -> 50.1 us (level)
  no operation moved by 1% of the time
where the time goes in v3:
time: 50.1 us; the launch traced here: 49.9 us
  Pallas kernels  43 us (86%)
  local copies, waits for them, and re-layouts  6.22 us (12%)
  between operations  0.68 us (1%)
    pallas_call x1, Pallas kernels, on_device_fused(): pl.pallas_call(functools.partial(step_kernel, dims), out_shape=(jax.Shape...  43 us
    unnamed x12, local copies, waits for them, and re-layouts  6.22 us

profile of v3, /device:TPU:0, one launch (start us, length us, event | category | flops | bytes accessed | tf_op | source)
XLA Modules:
  0.0 49.9 jit_solution(15737350406406434957)
XLA Ops:
  0.6 0.0 copy-start
  0.6 1.5 %copy.6.cot = bf16[512,608]{1,0:T(8,128)(2,1)S(1)} copy(bf16[512,608]{0,1:T(8,128)(2,1)} %param.5) | data formatting | bytes 1245184 | tf_op args[2]
  2.1 0.0 copy-done
  2.1 0.0 copy-start.3
  2.1 0.9 %copy-done.3 = bf16[32,5,608]{2,0,1:T(8,128)(2,1)S(1)} copy-done((bf16[32,5,608]{2,0,1:T(8,128)(2,1)S(1)}, bf16[32,5,608]{2,0,1:T(8,128)(2,1)}, u32[]{:S(2)}) %copy-start.3) | copy-done | bytes 194584
  3.0 43.0 %shard_map.58 = (bf16[512,608]{1,0:T(8,128)(2,1)S(1)}, bf16[1024,512]{1,0:T(8,128)(2,1)S(1)}, f32[5,32,608]{2,1,0:T(8,128)S(1)}) custom-call(bf16[1024,512]{1,0:T(8,128)(2,1)S(1)} %copy-done, bf16[5,2,16,608]{3,2,1,0:T(8,128)(2,1)S(1)} %bitcast.5, bf16[512,608]{1,0:T(8,128)(2,1)S(1)} %copy.6.cot), custom_call_target="tpu_custom_call" | custom-call | tf_op jit(solution)/shard_map/pallas_call | solution.py:383
  46.0 0.0 copy-start.1
  46.0 0.7 %copy-done.1 = f32[5,32,608]{2,1,0:T(8,128)} copy-done((f32[5,32,608]{2,1,0:T(8,128)}, f32[5,32,608]{2,1,0:T(8,128)S(1)}, u32[]{:S(2)}) %copy-start.1) | copy-done | bytes 389144
  46.8 1.1 %copy.7 = bf16[512,608]{0,1:T(8,128)(2,1)} copy(bf16[512,608]{1,0:T(8,128)(2,1)S(1)} %get-tuple-element.9) | data formatting | bytes 1245184
  47.9 0.0 copy-start.2
  47.9 1.0 %copy.10 = bf16[1024,512]{1,0:T(8,128)(2,1)} copy(bf16[1024,512]{1,0:T(8,128)(2,1)S(1)} %get-tuple-element.16) | data formatting | bytes 2097152
  48.8 0.3 copy-done.2
  49.1 0.8 %copy.11 = f32[32,5,608]{2,0,1:T(8,128)} copy(f32[32,5,608]{2,0,1:T(8,128)S(1)} %bitcast.4) | data formatting | bytes 778240
Async XLA Ops:
  0.6 1.5 %copy-start = (bf16[1024,512]{1,0:T(8,128)(2,1)S(1)}, bf16[1024,512]{1,0:T(8,128)(2,1)}, u32[]{:S(2)}) copy-start(bf16[1024,512]{1,0:T(8,128)(2,1)} %act.1) | copy-start | bytes 3145732
  2.1 0.9 %copy-start.3 = (bf16[32,5,608]{2,0,1:T(8,128)(2,1)S(1)}, bf16[32,5,608]{2,0,1:T(8,128)(2,1)}, u32[]{:S(2)}) copy-start(bf16[32,5,608]{2,0,1:T(8,128)(2,1)} %param.4) | copy-start | bytes 583684
  46.0 0.8 %copy-start.1 = (f32[5,32,608]{2,1,0:T(8,128)}, f32[5,32,608]{2,1,0:T(8,128)S(1)}, u32[]{:S(2)}) copy-start(f32[5,32,608]{2,1,0:T(8,128)S(1)} %get-tuple-element.8) | copy-start | bytes 1167364
  47.9 1.3 %copy-start.2 = (f32[5,32,608]{2,1,0:T(8,128)S(1)}, f32[5,32,608]{2,1,0:T(8,128)}, u32[]{:S(2)}) copy-start(f32[5,32,608]{2,1,0:T(8,128)} %copy-done.1) | copy-start | bytes 1167364

commit v4 on v3

--- a/solution.py
+++ b/solution.py
@@ -300,9 +300,10 @@
         tap_dot(k)
         if k:
             tap_core(k - 1)
-        if k < len(arrivals):
-            take_z(*arrivals[k])
+        if 0 < k < len(arrivals):
+            take_z(*arrivals[k - 1])
     tap_core(taps - 1)
+    take_z(3, 0)
     take_z(3, 1)
     gl.wait_recv()
     gr.wait_recv()

time: 50.1 us -> 49.6 us (0.990)
    pallas_call x1, Pallas kernels: 43 us -> 42.5 us  [on_device_fused(): pl.pallas_call(functools.partial(step_kernel, dims), out_shape=(jax.Shape...]
where the time goes in v4:
time: 49.6 us; the launch traced here: 49.4 us
  Pallas kernels  42.5 us (86%)
  local copies, waits for them, and re-layouts  6.22 us (13%)
  between operations  0.68 us (1%)
    pallas_call x1, Pallas kernels, on_device_fused(): pl.pallas_call(functools.partial(step_kernel, dims), out_shape=(jax.Shape...  42.5 us
    unnamed x12, local copies, waits for them, and re-layouts  6.22 us

profile of v4, /device:TPU:0, one launch (start us, length us, event | category | flops | bytes accessed | tf_op | source)
XLA Modules:
  0.0 49.4 jit_solution(10306995176447232637)
XLA Ops:
  0.6 0.0 copy-start
  0.6 1.5 %copy.6.cot = bf16[512,608]{1,0:T(8,128)(2,1)S(1)} copy(bf16[512,608]{0,1:T(8,128)(2,1)} %param.5) | data formatting | bytes 1245184 | tf_op args[2]
  2.1 0.0 copy-done
  2.1 0.0 copy-start.3
  2.1 0.9 %copy-done.3 = bf16[32,5,608]{2,0,1:T(8,128)(2,1)S(1)} copy-done((bf16[32,5,608]{2,0,1:T(8,128)(2,1)S(1)}, bf16[32,5,608]{2,0,1:T(8,128)(2,1)}, u32[]{:S(2)}) %copy-start.3) | copy-done | bytes 194584
  3.0 42.5 %shard_map.58 = (bf16[512,608]{1,0:T(8,128)(2,1)S(1)}, bf16[1024,512]{1,0:T(8,128)(2,1)S(1)}, f32[5,32,608]{2,1,0:T(8,128)S(1)}) custom-call(bf16[1024,512]{1,0:T(8,128)(2,1)S(1)} %copy-done, bf16[5,2,16,608]{3,2,1,0:T(8,128)(2,1)S(1)} %bitcast.5, bf16[512,608]{1,0:T(8,128)(2,1)S(1)} %copy.6.cot), custom_call_target="tpu_custom_call" | custom-call | tf_op jit(solution)/shard_map/pallas_call | solution.py:384
  45.5 0.0 copy-start.1
  45.5 0.7 %copy-done.1 = f32[5,32,608]{2,1,0:T(8,128)} copy-done((f32[5,32,608]{2,1,0:T(8,128)}, f32[5,32,608]{2,1,0:T(8,128)S(1)}, u32[]{:S(2)}) %copy-start.1) | copy-done | bytes 389144
  46.3 1.1 %copy.7 = bf16[512,608]{0,1:T(8,128)(2,1)} copy(bf16[512,608]{1,0:T(8,128)(2,1)S(1)} %get-tuple-element.9) | data formatting | bytes 1245184
  47.3 0.0 copy-start.2
  47.3 1.0 %copy.10 = bf16[1024,512]{1,0:T(8,128)(2,1)} copy(bf16[1024,512]{1,0:T(8,128)(2,1)S(1)} %get-tuple-element.16) | data formatting | bytes 2097152
  48.3 0.3 copy-done.2
  48.6 0.8 %copy.11 = f32[32,5,608]{2,0,1:T(8,128)} copy(f32[32,5,608]{2,0,1:T(8,128)S(1)} %bitcast.4) | data formatting | bytes 778240
Async XLA Ops:
  0.6 1.5 %copy-start = (bf16[1024,512]{1,0:T(8,128)(2,1)S(1)}, bf16[1024,512]{1,0:T(8,128)(2,1)}, u32[]{:S(2)}) copy-start(bf16[1024,512]{1,0:T(8,128)(2,1)} %act.1) | copy-start | bytes 3145732
  2.1 0.9 %copy-start.3 = (bf16[32,5,608]{2,0,1:T(8,128)(2,1)S(1)}, bf16[32,5,608]{2,0,1:T(8,128)(2,1)}, u32[]{:S(2)}) copy-start(bf16[32,5,608]{2,0,1:T(8,128)(2,1)} %param.4) | copy-start | bytes 583684
  45.5 0.8 %copy-start.1 = (f32[5,32,608]{2,1,0:T(8,128)}, f32[5,32,608]{2,1,0:T(8,128)S(1)}, u32[]{:S(2)}) copy-start(f32[5,32,608]{2,1,0:T(8,128)S(1)} %get-tuple-element.8) | copy-start | bytes 1167364
  47.3 1.3 %copy-start.2 = (f32[5,32,608]{2,1,0:T(8,128)S(1)}, f32[5,32,608]{2,1,0:T(8,128)}, u32[]{:S(2)}) copy-start(f32[5,32,608]{2,1,0:T(8,128)} %copy-done.1) | copy-start | bytes 1167364
